TPU v7x, 256 devices: a whole 4x4x8 slice. The times are simulated.
256 devices in a mesh: box: 16 (over y_lo, z), theta: 4 (over y_hi, core), phi: 4 (over x).
Axes of the slice: x: 4, y: 4 (y_hi: 2, y_lo: 2; y = y_hi * 2 + y_lo), z: 8, core: 2. Of those that a mesh axis runs over, the one named last changes fastest.
Arguments:
- coeffs: bfloat16 [2048, 2, 128, 256], P(('box', 'theta', 'phi')), may hold values from -6 to 6
- near_blocks: bfloat16 [2048, 12, 2, 128, 128], P(('box', 'theta', 'phi')), may hold values from -0.109375 to 0.109375
- near_ids: int32 [2048, 12], P(('box', 'theta', 'phi')), may hold values from 0 to 2047, as said below
- near_count: int32 [2048], P(('box', 'theta', 'phi')), may hold values from 3 to 12, as said below
- radiation: bfloat16 [2048, 2, 128, 128], P(('box', 'theta', 'phi')), may hold values from -0.5 to 0.5
- partners: int32 [256, 16], P('box'), may hold values from 0 to 255, as said below
- vector_ids: int32 [256, 16], P('box'), may hold values from 0 to 315
- pair_count: int32 [256], P('box'), may hold values from 4 to 16, as said below
- translation: bfloat16 [316, 2, 16, 32], P(None, None, 'theta', 'phi'), may hold values from -0.5 to 0.5
Outputs:
- product: float32 [2048, 2, 128, 256], P(('box', 'theta', 'phi'))
Inputs may be any that keep to these rules, and one draw needn't show every extreme that they name: `near_ids`: row b lists b itself first, then 12 - 1 further entries; the used ones (before near_count[b]) are distinct other leaf boxes whose index differs from b by at most 8, and some used entry differs by exactly 8. Entries at or after near_count[b] are not used and may repeat b. `near_count`: some leaf box uses all 12 slots. `partners`: row d holds 16 distinct upper boxes other than d whose index differs from d by at most 16; a difference of exactly 16 occurs among used entries. Entries at or after pair_count[d] are not used. `pair_count`: some upper box uses all 16 slots.
All inputs are finite; a program needn't handle non-finite values.
Results may differ from a plain program's by a relative error of at most 0.0055.
Values may be sent and summed in bfloat16 or wider, within the bound.
A program may use at most 128 MiB of HBM per device.

v0:
```python
import math

import jax
import jax.numpy as jnp
from jax import lax
from jax.sharding import PartitionSpec as P

TL = 8
PL = 16
TU = 16
PU = 32


WEIGHT_UP = (-0.0546875, 0.8203125, 0.2734375, -0.0390625)
WEIGHT_DOWN = (-0.0390625, 0.2734375, 0.8203125, -0.0546875)
PHASE_SCALE = 1.3


def padded(block, sides, width):
    for axis, dim in sides:
        count = lax.axis_size(axis)
        forward = [(i, i + 1) for i in range(count - 1)]
        backward = [(target, source) for source, target in forward]
        low = lax.ppermute(
            lax.slice_in_dim(block, block.shape[dim] - width, None, axis=dim), axis, forward
        )
        high = lax.ppermute(lax.slice_in_dim(block, 0, width, axis=dim), axis, backward)
        block = jnp.concatenate([low, block, high], axis=dim)
    return block


def lagrange_matrix(upper, columns, rows_in, mode, shift):
    halves = upper // 2
    parity = upper % 2
    column_ids = jnp.arange(columns)
    matrix = jnp.zeros((upper.shape[0], columns), jnp.float32)
    for order in range(4):
        node = halves + parity - 2 + order
        if mode == "wrap":
            node = node % rows_in
        else:
            node = jnp.clip(node, 0, rows_in - 1)
        node = node - shift
        weight = jnp.where(parity == 1, WEIGHT_UP[order], WEIGHT_DOWN[order]).astype(jnp.float32)
        matrix = matrix + weight[:, None] * (column_ids[None, :] == node[:, None]).astype(
            jnp.float32
        )
    return matrix


def phases(theta_ids, phi_ids, theta_total, phi_total):
    theta = math.pi * (theta_ids.astype(jnp.float32) + 0.5) / theta_total
    azimuth = 2.0 * math.pi * (phi_ids.astype(jnp.float32) + 0.5) / phi_total
    octant = jnp.arange(8)
    sign_x = (2 * (octant % 2) - 1).astype(jnp.float32)[:, None, None]
    sign_y = (2 * (octant // 2 % 2) - 1).astype(jnp.float32)[:, None, None]
    sign_z = (2 * (octant // 4) - 1).astype(jnp.float32)[:, None, None]
    along_x = (jnp.sin(theta)[:, None] * jnp.cos(azimuth)[None, :])[None]
    along_y = (jnp.sin(theta)[:, None] * jnp.sin(azimuth)[None, :])[None]
    along_z = (jnp.cos(theta)[:, None] * jnp.ones_like(azimuth)[None, :])[None]
    angle = PHASE_SCALE * (sign_x * along_x + sign_y * along_y + sign_z * along_z)
    return (jnp.cos(angle), jnp.sin(angle))


def per_device(
    coeffs,
    near_blocks,
    near_ids,
    near_count,
    radiation,
    partners,
    vector_ids,
    pair_count,
    translation,
):
    highest = lax.Precision.HIGHEST
    boxes_here = coeffs.shape[0]
    rhs_count = coeffs.shape[3]
    slot_total = near_ids.shape[1]
    leaf_rank = lax.axis_index(("box", "theta", "phi"))
    widened = padded(coeffs, ((("box", "theta", "phi"), 0),), boxes_here)
    local_ids = near_ids - (leaf_rank * boxes_here - boxes_here)
    slot_ids = jnp.arange(slot_total)
    picked = widened[local_ids]
    in_use = slot_ids[None, :] < near_count[:, None]
    picked = jnp.where(in_use[:, :, None, None, None], picked, jnp.zeros((), picked.dtype))
    near_real = jnp.einsum(
        "bjpq,bjqr->bpr", near_blocks[:, :, 0], picked[:, :, 0], preferred_element_type=jnp.float32
    ) - jnp.einsum(
        "bjpq,bjqr->bpr", near_blocks[:, :, 1], picked[:, :, 1], preferred_element_type=jnp.float32
    )
    near_imag = jnp.einsum(
        "bjpq,bjqr->bpr", near_blocks[:, :, 0], picked[:, :, 1], preferred_element_type=jnp.float32
    ) + jnp.einsum(
        "bjpq,bjqr->bpr", near_blocks[:, :, 1], picked[:, :, 0], preferred_element_type=jnp.float32
    )
    near_field = jnp.stack([near_real, near_imag], axis=1)
    pattern_real = jnp.einsum(
        "bkp,bpr->bkr", radiation[:, 0], coeffs[:, 0], preferred_element_type=jnp.float32
    ) - jnp.einsum(
        "bkp,bpr->bkr", radiation[:, 1], coeffs[:, 1], preferred_element_type=jnp.float32
    )
    pattern_imag = jnp.einsum(
        "bkp,bpr->bkr", radiation[:, 0], coeffs[:, 1], preferred_element_type=jnp.float32
    ) + jnp.einsum(
        "bkp,bpr->bkr", radiation[:, 1], coeffs[:, 0], preferred_element_type=jnp.float32
    )
    leaf_pattern = jnp.stack([pattern_real, pattern_imag], axis=1).astype(jnp.bfloat16)
    theta_size = lax.axis_size("theta")
    phi_size = lax.axis_size("phi")
    groups = theta_size * phi_size
    theta_band = TU // theta_size
    phi_band = PU // phi_size
    full_theta = lagrange_matrix(jnp.arange(TU), TL, TL, "clamp", 0)
    full_phi = lagrange_matrix(jnp.arange(PU), PL, PL, "wrap", 0)
    cosine_full, sine_full = phases(jnp.arange(TU), jnp.arange(PU), TU, PU)
    cosine_full = cosine_full[:, :, :, None]
    sine_full = sine_full[:, :, :, None]
    grid = leaf_pattern.reshape(boxes_here, 2, TL, PL, rhs_count)
    partial_up = jnp.einsum(
        "ut,bctlr->bculr", full_theta.astype(jnp.bfloat16), grid, preferred_element_type=jnp.float32
    )
    refined = jnp.einsum("vl,bculr->bcuvr", full_phi, partial_up, precision=highest)
    shifted_real = cosine_full * refined[:, 0] - sine_full * refined[:, 1]
    shifted_imag = sine_full * refined[:, 0] + cosine_full * refined[:, 1]
    parent = jnp.stack([jnp.sum(shifted_real, axis=0), jnp.sum(shifted_imag, axis=0)]).astype(
        jnp.bfloat16
    )
    spread = parent.reshape(2, theta_size, theta_band, phi_size, phi_band, rhs_count)
    spread = spread.transpose(1, 3, 0, 2, 4, 5).reshape(groups, 2, theta_band, phi_band, rhs_count)
    bands = lax.all_to_all(spread, ("theta", "phi"), split_axis=0, concat_axis=0, tiled=True)
    per_group = bands.shape[0]
    samples = theta_band * phi_band
    group_rank = lax.axis_index("box")
    operator_total = translation.shape[0]
    list_total = vector_ids.shape[1]
    selector = (vector_ids[:, :, None] == jnp.arange(operator_total)[None, None, :]).astype(
        jnp.bfloat16
    )
    table = translation.reshape(operator_total, 2 * samples)
    chosen = jnp.einsum("dmv,vs->dms", selector, table, preferred_element_type=jnp.float32)
    in_list = jnp.arange(list_total)[None, :] < pair_count[:, None]
    chosen = jnp.where(in_list[:, :, None], chosen, 0.0).astype(jnp.bfloat16)
    reach = padded(bands, (("box", 0),), per_group)
    width_here = reach.shape[0]
    matches = (
        partners[:, :, None]
        == group_rank * per_group - per_group + jnp.arange(width_here)[None, None, :]
    ).astype(jnp.bfloat16)
    coupling = jnp.einsum(
        "dmj,dms->sdj", matches, chosen, preferred_element_type=jnp.float32
    ).astype(jnp.bfloat16)
    coupling = coupling.reshape(2, samples, per_group, width_here)
    flat = reach.reshape(width_here, 2, samples, rhs_count)
    out_real = jnp.einsum(
        "sdj,jsr->dsr", coupling[0], flat[:, 0], preferred_element_type=jnp.float32
    ) - jnp.einsum("sdj,jsr->dsr", coupling[1], flat[:, 1], preferred_element_type=jnp.float32)
    out_imag = jnp.einsum(
        "sdj,jsr->dsr", coupling[0], flat[:, 1], preferred_element_type=jnp.float32
    ) + jnp.einsum("sdj,jsr->dsr", coupling[1], flat[:, 0], preferred_element_type=jnp.float32)
    field = jnp.stack([out_real, out_imag], axis=1)
    incoming = field.reshape(per_group, 2, theta_band, phi_band, rhs_count).astype(jnp.bfloat16)
    returned = lax.all_to_all(incoming, ("theta", "phi"), split_axis=0, concat_axis=0, tiled=True)
    whole = returned.reshape(theta_size, phi_size, 2, theta_band, phi_band, rhs_count)
    whole = whole.transpose(2, 0, 3, 1, 4, 5).reshape(2, TU, PU, rhs_count).astype(jnp.float32)
    down_real = cosine_full * whole[0][None] + sine_full * whole[1][None]
    down_imag = cosine_full * whole[1][None] - sine_full * whole[0][None]
    spread_down = jnp.stack([down_real, down_imag], axis=1)
    coarse_phi = jnp.einsum("vl,bcuvr->bculr", full_phi, spread_down, precision=highest)
    leaf_field = jnp.einsum("ut,bculr->bctlr", full_theta, coarse_phi, precision=highest).astype(
        jnp.bfloat16
    )
    leaf_field = leaf_field.reshape(boxes_here, 2, TL * PL, rhs_count)
    far_real = jnp.einsum(
        "bkp,bkr->bpr", radiation[:, 0], leaf_field[:, 0], preferred_element_type=jnp.float32
    ) + jnp.einsum(
        "bkp,bkr->bpr", radiation[:, 1], leaf_field[:, 1], preferred_element_type=jnp.float32
    )
    far_imag = jnp.einsum(
        "bkp,bkr->bpr", radiation[:, 0], leaf_field[:, 1], preferred_element_type=jnp.float32
    ) - jnp.einsum(
        "bkp,bkr->bpr", radiation[:, 1], leaf_field[:, 0], preferred_element_type=jnp.float32
    )
    return near_field + jnp.stack([far_real, far_imag], axis=1)


def solution(mesh):
    in_specs = (
        P(("box", "theta", "phi"), None, None, None),
        P(("box", "theta", "phi"), None, None, None, None),
        P(("box", "theta", "phi"), None),
        P(("box", "theta", "phi")),
        P(("box", "theta", "phi"), None, None, None),
        P("box", None),
        P("box", None),
        P("box"),
        P(None, None, "theta", "phi"),
    )
    out_specs = P(("box", "theta", "phi"), None, None, None)
    return jax.shard_map(
        per_device, mesh=mesh, in_specs=in_specs, out_specs=out_specs, check_vma=False
    )
```

profile of v0, /device:TPU:26, one launch (start us, length us, event | category | flops | bytes accessed | tf_op | source)
XLA Modules:
  0.0 138.0 jit_solution(5881483074914443339)
XLA Ops:
  0.0 2.6 %collective-permute-start.1 = (bf16[8,2,128,256]{3,2,1,0:T(8,128)(2,1)}, bf16[8,2,128,256]{3,2,1,0:T(8,128)(2,1)S(1)}, u32[]{:S(2)}, u32[]{:S(2)}) collective-permute-start(bf16[8,2,128,256]{3,2,1,0:T(8,128)(2,1)} %param.9), channel_id=1, source_target_pairs={{1,0},{2,1},{3,2},{4,3},{5,4},{6,5},{7,6},{8,7},{9,8},{10,9},{11,1... | collective-permute-start | bytes 3145736 | tf_op jit(solution)/shard_map/ppermute | solution.py:27
  2.6 3.4 %collective-permute-start = (bf16[8,2,128,256]{3,2,1,0:T(8,128)(2,1)}, bf16[8,2,128,256]{3,2,1,0:T(8,128)(2,1)}, u32[]{:S(2)}, u32[]{:S(2)}) collective-permute-start(bf16[8,2,128,256]{3,2,1,0:T(8,128)(2,1)} %param.9), channel_id=1, source_target_pairs={{0,1},{1,2},{2,3},{3,4},{4,5},{5,6},{6,7},{7,8},{8,9},{9,10},{10,1... | collective-permute-start | bytes 3145736 | tf_op jit(solution)/shard_map/ppermute | solution.py:24
  6.0 1.4 %fusion.69 = f32[8,128,256]{2,1,0:T(8,128)S(1)} fusion(bf16[8,2,128,256]{3,2,1,0:T(8,128)(2,1)} %param.9, bf16[8,2,128,128]{3,2,1,0:T(8,128)(2,1)} %param.13), kind=kOutput, calls=%fused_computation.74 | convolution fusion | flops 67108864 | bytes 1835008 | tf_op jit(solution)/shard_map/bkp,bpr->bkr/dot_general | solution.py:103
  7.4 1.4 %fusion.73 = f32[8,128,256]{2,1,0:T(8,128)S(1)} fusion(bf16[8,2,128,256]{3,2,1,0:T(8,128)(2,1)} %param.9, bf16[8,2,128,128]{3,2,1,0:T(8,128)(2,1)} %param.13), kind=kOutput, calls=%fused_computation.78 | convolution fusion | flops 67108864 | bytes 1835008 | tf_op jit(solution)/shard_map/bkp,bpr->bkr/dot_general | solution.py:98
  9.1 1.4 %fusion.59 = bf16[8,128,256]{2,1,0:T(8,128)(2,1)S(1)} fusion(f32[8,128,256]{2,1,0:T(8,128)S(1)} %fusion.69, bf16[8,2,128,256]{3,2,1,0:T(8,128)(2,1)} %param.9, bf16[8,2,128,128]{3,2,1,0:T(8,128)(2,1)} %param.13), kind=kOutput, calls=%fused_computation.53 | convolution fusion | flops 67633152 | bytes 2359296 | tf_op jit(solution)/shard_map/bkp,bpr->bkr/dot_general | solution.py:105
  10.5 0.2 copy.47
  10.7 0.3 fusion.58
  11.0 0.2 copy.46
  11.3 0.3 fusion.104
  11.6 0.8 convolution_bitcast_fusion
  12.4 9.2 %fusion.12 = f32[8,2,16,32,256]{4,3,2,1,0:T(8,128)S(1)} fusion(f32[8,2,16,16,256]{4,2,3,1,0:T(8,128)S(1)} %convolution_bitcast_fusion, f32[32]{0:T(128)S(1)} %get-tuple-element.31, s32[32]{0:T(128)S(1)} %get-tuple-element.25, f32[32]{0:T(128)S(1)} %get-tuple-element.29, s32[32]{0:T(128)S(1)} %get-tuple-element.26, f32[32]{0:T(128)S(1)} %get-tuple-element.30, ...), kind=kOutput, calls=%fused_computation.22 | convolution fusion | flops 402658816 | bytes 12583936 | tf_op jit(solution)/shard_map/vl,bculr->bcuvr/dot_general | solution.py:123
  21.6 1.8 %subtract_reduce_fusion = (bf16[16,32,256]{2,1,0:T(8,128)(2,1)S(1)}, bf16[16,32,256]{2,1,0:T(8,128)(2,1)S(1)}) fusion(f32[8,2,16,32,256]{4,3,2,1,0:T(8,128)S(1)} %fusion.12, f32[8,16,32]{2,1,0:T(8,128)S(1)} %get-tuple-element.14, f32[8,16,32]{2,1,0:T(8,128)S(1)} %get-tuple-element.13), kind=kLoop, calls=%fused_computation.21 | loop fusion | flops 8126464 | bytes 8945664 | tf_op jit(solution)/shard_map/reduce_sum | solution.py:126
  23.5 0.9 copy.50
  24.3 11.1 %all-to-all-start = ((bf16[16,2,4,8,256]{4,3,2,1,0:T(8,128)(2,1)}), bf16[16,2,4,8,256]{4,3,2,1,0:T(8,128)(2,1)S(1)}, u32[]{:S(2)}, u32[]{:S(2)}) async-start(bf16[16,2,4,8,256]{4,3,2,1,0:T(8,128)(2,1)} %bitcast.34), calls=%async_computation | async-start | bytes 1048576 | tf_op jit(solution)/shard_map/all_to_all | solution.py:131
  35.7 0.5 fusion.62
  36.1 7.6 %all-to-all-done = bf16[16,2,4,8,256]{4,3,2,1,0:T(8,128)(2,1)S(1)} async-done(((bf16[16,2,4,8,256]{4,3,2,1,0:T(8,128)(2,1)}), bf16[16,2,4,8,256]{4,3,2,1,0:T(8,128)(2,1)S(1)}, u32[]{:S(2)}, u32[]{:S(2)}) %all-to-all-start) | async-done | bytes 524320 | tf_op jit(solution)/shard_map/all_to_all | solution.py:131
  43.8 7.2 %collective-permute-start.3 = (bf16[16,2,4,8,256]{4,3,2,1,0:T(8,128)(2,1)S(1)}, bf16[16,2,4,8,256]{4,3,2,1,0:T(8,128)(2,1)S(1)}, u32[]{:S(2)}, u32[]{:S(2)}) collective-permute-start(bf16[16,2,4,8,256]{4,3,2,1,0:T(8,128)(2,1)S(1)} %all-to-all-done), channel_id=1, source_target_pairs={{16,0},{32,16},{48,32},{64,48},{80,64},{96,80},{112,96},{128,112},... | collective-permute-start | bytes 1572872 | tf_op jit(solution)/shard_map/ppermute | solution.py:27
  51.0 1.9 %collective-permute-start.2 = (bf16[16,2,4,8,256]{4,3,2,1,0:T(8,128)(2,1)S(1)}, bf16[16,2,4,8,256]{4,3,2,1,0:T(8,128)(2,1)}, u32[]{:S(2)}, u32[]{:S(2)}) collective-permute-start(bf16[16,2,4,8,256]{4,3,2,1,0:T(8,128)(2,1)S(1)} %all-to-all-done), channel_id=1, source_target_pairs={{0,16},{16,32},{32,48},{48,64},{64,80},{80,96},{96,112},{112,128},... | collective-permute-start | bytes 1572872 | tf_op jit(solution)/shard_map/ppermute | solution.py:24
  53.5 9.2 %collective-permute-done.3 = bf16[16,2,4,8,256]{4,3,2,1,0:T(8,128)(2,1)S(1)} collective-permute-done((bf16[16,2,4,8,256]{4,3,2,1,0:T(8,128)(2,1)S(1)}, bf16[16,2,4,8,256]{4,3,2,1,0:T(8,128)(2,1)S(1)}, u32[]{:S(2)}, u32[]{:S(2)}) %collective-permute-start.3) | collective-permute-done | bytes 524320 | tf_op jit(solution)/shard_map/ppermute | solution.py:27
  62.7 6.3 %collective-permute-done.2 = bf16[16,2,4,8,256]{4,3,2,1,0:T(8,128)(2,1)} collective-permute-done((bf16[16,2,4,8,256]{4,3,2,1,0:T(8,128)(2,1)S(1)}, bf16[16,2,4,8,256]{4,3,2,1,0:T(8,128)(2,1)}, u32[]{:S(2)}, u32[]{:S(2)}) %collective-permute-start.2) | collective-permute-done | bytes 524320 | tf_op jit(solution)/shard_map/ppermute | solution.py:24
  69.0 1.2 pad_maximum_fusion.1
  70.2 0.9 copy.51
  71.1 0.2 fusion.68
  71.4 0.2 fusion.61
  71.7 0.2 fusion.67
  71.9 0.2 fusion.60
  72.3 0.8 pad_maximum_fusion.2
  73.1 7.1 %all-to-all-start.1 = ((bf16[16,2,4,8,256]{4,3,2,1,0:T(8,128)(2,1)}), bf16[16,2,4,8,256]{4,3,2,1,0:T(8,128)(2,1)}, u32[]{:S(2)}, u32[]{:S(2)}) async-start(bf16[16,2,4,8,256]{4,3,2,1,0:T(8,128)(2,1)} %pad_maximum_fusion.2), calls=%async_computation.1 | async-start | bytes 1048576 | tf_op jit(solution)/shard_map/all_to_all | solution.py:163
  80.2 1.0 copy-done.5
  81.2 2.0 %pad_maximum_fusion = bf16[24,2,128,256]{3,2,1,0:T(8,128)(2,1)S(1)} fusion(bf16[8,2,128,256]{3,2,1,0:T(8,128)(2,1)} %copy-done.5, bf16[8,2,128,256]{3,2,1,0:T(8,128)(2,1)} %param.9, bf16[8,2,128,256]{3,2,1,0:T(8,128)(2,1)} %collective-permute-done), kind=kLoop, calls=%fused_computation.23 | loop fusion | flops 3145728 | bytes 6291456 | tf_op jit(solution)/shard_map/concatenate | solution.py:28
  83.2 6.8 %gather_fusion = bf16[96,2,128,256]{3,2,1,0:T(8,128)(2,1)} fusion(bf16[24,2,128,256]{3,2,1,0:T(8,128)(2,1)S(1)} %pad_maximum_fusion, s32[1024]{0:T(1024)S(1)} %pad_clamp_fusion), kind=kCustom, calls=%fused_computation | custom fusion | bytes 25166208 | tf_op jit(solution)/shard_map/gather | solution.py:84
  90.1 16.9 %copy.39 = bf16[96,2,128,256]{2,3,0,1:T(8,128)(2,1)} copy(bf16[96,2,128,256]{3,2,1,0:T(8,128)(2,1)} %gather_fusion) | data formatting | bytes 25165824 | tf_op jit(solution)/shard_map/gather | solution.py:84
  107.0 6.6 %broadcast_select_fusion = bf16[8,12,2,128,256]{3,4,1,0,2:T(8,128)(2,1)S(1)} fusion(bf16[8,12,2,128,256]{3,4,1,0,2:T(8,128)(2,1)} %bitcast.218, pred[8,12]{1,0:T(8,128)(4,1)S(1)} %iota_compare_fusion.12), kind=kLoop, calls=%fused_computation.1 | loop fusion | flops 6291456 | bytes 25165920 | tf_op jit(solution)/shard_map/jit(_where)/select_n | solution.py:86
  113.6 1.8 %fusion.35 = f32[8,256,128]{2,1,0:T(8,128)S(1)} fusion(bf16[8,12,2,128,128]{4,3,2,1,0:T(8,128)(2,1)S(1)} %bitcast.236, bf16[8,12,2,128,256]{3,4,1,0,2:T(8,128)(2,1)S(1)} %broadcast_select_fusion), kind=kOutput, calls=%fused_computation.39 | convolution fusion | flops 805306368 | bytes 10485760 | tf_op jit(solution)/shard_map/bjpq,bjqr->bpr/dot_general | solution.py:92
  115.4 1.8 %fusion.32 = f32[8,256,128]{2,1,0:T(8,128)S(1)} fusion(bf16[8,12,2,128,128]{4,3,2,1,0:T(8,128)(2,1)S(1)} %bitcast.236, bf16[8,12,2,128,256]{3,4,1,0,2:T(8,128)(2,1)S(1)} %broadcast_select_fusion), kind=kOutput, calls=%fused_computation.38 | convolution fusion | flops 805306368 | bytes 10485760 | tf_op jit(solution)/shard_map/bjpq,bjqr->bpr/dot_general | solution.py:89
  117.1 1.8 %fusion.49 = f32[8,1,128,256]{2,3,0,1:T(8,128)S(1)} fusion(f32[8,256,128]{2,1,0:T(8,128)S(1)} %fusion.35, bf16[8,12,2,128,128]{4,3,2,1,0:T(8,128)(2,1)S(1)} %bitcast.236, bf16[8,12,2,128,256]{3,4,1,0,2:T(8,128)(2,1)S(1)} %broadcast_select_fusion), kind=kOutput, calls=%fused_computation.49 | convolution fusion | flops 805568512 | bytes 11534336 | tf_op jit(solution)/shard_map/bjpq,bjqr->bpr/dot_general | solution.py:94
  118.9 2.8 %fusion.55 = f32[8,1,128,256]{2,3,0,1:T(8,128)} fusion(f32[8,256,128]{2,1,0:T(8,128)S(1)} %fusion.32, bf16[8,12,2,128,128]{4,3,2,1,0:T(8,128)(2,1)S(1)} %bitcast.236, bf16[8,12,2,128,256]{3,4,1,0,2:T(8,128)(2,1)S(1)} %broadcast_select_fusion), kind=kOutput, calls=%fused_computation.51 | convolution fusion | flops 805568512 | bytes 11534336 | tf_op jit(solution)/shard_map/bjpq,bjqr->bpr/dot_general | solution.py:87
  121.7 1.1 convert_bitcast_fusion
  123.1 1.5 %multiply_add_fusion = (f32[8,1,16,32,256]{4,3,2,1,0:T(8,128)S(1)}, f32[8,1,16,32,256]{4,3,2,1,0:T(8,128)S(1)}) fusion(f32[16,32,256]{2,1,0:T(8,128)S(1)} %bitcast.227, f32[8,16,32]{2,1,0:T(8,128)S(1)} %get-tuple-element.14, f32[16,32,256]{2,1,0:T(8,128)S(1)} %bitcast.228, f32[8,16,32]{2,1,0:T(8,128)S(1)} %get-tuple-element.13), kind=kLoop, calls=%fused_computation.19 | loop fusion | flops 6291456 | bytes 9469952 | tf_op jit(solution)/shard_map/add | solution.py:166
  124.6 4.8 %fusion.23 = f32[8,2,16,16,256]{4,3,2,1,0:T(8,128)S(1)} fusion(f32[8,1,16,32,256]{4,3,2,1,0:T(8,128)S(1)} %get-tuple-element.8, f32[8,1,16,32,256]{4,3,2,1,0:T(8,128)S(1)} %get-tuple-element.7, f32[32]{0:T(128)S(1)} %get-tuple-element.31, s32[32]{0:T(128)S(1)} %get-tuple-element.25, f32[32]{0:T(128)S(1)} %get-tuple-element.29, ...), kind=kOutput, calls=%fused_computation.32 | convolution fusion | flops 404755968 | bytes 12583936 | tf_op jit(solution)/shard_map/vl,bcuvr->bculr/dot_general | solution.py:169
  129.4 4.7 %fusion.29 = bf16[8,2,8,16,256]{4,2,3,1,0:T(8,128)(2,1)S(1)} fusion(f32[8,2,16,16,256]{4,3,2,1,0:T(8,128)S(1)} %fusion.23, f32[16]{0:T(128)S(1)} %get-tuple-element.23, s32[16]{0:T(128)S(1)} %get-tuple-element.17, f32[16]{0:T(128)S(1)} %get-tuple-element.21, s32[16]{0:T(128)S(1)} %get-tuple-element.20, f32[16]{0:T(128)S(1)} %get-tuple-element.22, ...), kind=kOutput, calls=%fused_computation.37 | convolution fusion | flops 101188992 | bytes 5243392 | tf_op jit(solution)/shard_map/ut,bculr->bctlr/dot_general | solution.py:170
  134.1 0.2 copy.61
  134.3 0.3 fusion.76
  134.7 0.3 fusion.75
  135.0 0.3 fusion.44
  135.4 0.4 fusion.45
  135.9 0.2 maximum_add_fusion
  136.2 1.8 %copy.64 = f32[8,2,128,256]{3,2,1,0:T(8,128)} copy(f32[8,2,128,256]{2,3,0,1:T(8,128)S(1)} %maximum_add_fusion) | data formatting | bytes 4194304 | tf_op jit(solution)/shard_map/add | solution.py:184
  (60 shorter events, 1.6 us)
Async XLA Ops:
  0.0 35.6 %copy-start = (bf16[316,2,4,8]{0,3,2,1:T(8,128)(2,1)S(1)}, bf16[316,2,4,8]{0,3,2,1:T(8,128)(2,1)}, u32[]{:S(2)}) copy-start(bf16[316,2,4,8]{0,3,2,1:T(8,128)(2,1)} %param.17) | copy-start | bytes 121348
  0.0 10.7 %copy-start.2 = (bf16[8,2,128,256]{3,2,1,0:T(8,128)(2,1)S(1)}, bf16[8,2,128,256]{3,2,1,0:T(8,128)(2,1)}, u32[]{:S(2)}) copy-start(bf16[8,2,128,256]{3,2,1,0:T(8,128)(2,1)} %param.9) | copy-start | bytes 3145732
  0.0 10.7 %copy-start.3 = (bf16[8,2,128,128]{3,2,1,0:T(8,128)(2,1)S(1)}, bf16[8,2,128,128]{3,2,1,0:T(8,128)(2,1)}, u32[]{:S(2)}) copy-start(bf16[8,2,128,128]{3,2,1,0:T(8,128)(2,1)} %param.13) | copy-start | bytes 1572868
  0.0 80.2 %collective-permute-start.1 = (bf16[8,2,128,256]{3,2,1,0:T(8,128)(2,1)}, bf16[8,2,128,256]{3,2,1,0:T(8,128)(2,1)S(1)}, u32[]{:S(2)}, u32[]{:S(2)}) collective-permute-start(bf16[8,2,128,256]{3,2,1,0:T(8,128)(2,1)} %param.9), channel_id=1, source_target_pairs={{1,0},{2,1},{3,2},{4,3},{5,4},{6,5},{7,6},{8,7},{9,8},{10,9},{11,1... | collective-permute-start | bytes 3145736 | tf_op jit(solution)/shard_map/ppermute | solution.py:27
  2.6 78.6 %collective-permute-start = (bf16[8,2,128,256]{3,2,1,0:T(8,128)(2,1)}, bf16[8,2,128,256]{3,2,1,0:T(8,128)(2,1)}, u32[]{:S(2)}, u32[]{:S(2)}) collective-permute-start(bf16[8,2,128,256]{3,2,1,0:T(8,128)(2,1)} %param.9), channel_id=1, source_target_pairs={{0,1},{1,2},{2,3},{3,4},{4,5},{5,6},{6,7},{7,8},{8,9},{9,10},{10,1... | collective-permute-start | bytes 3145736 | tf_op jit(solution)/shard_map/ppermute | solution.py:24
  21.6 13.9 %copy-start.7 = (s32[8,12]{1,0:T(8,128)S(1)}, s32[8,12]{1,0:T(8,128)}, u32[]{:S(2)}) copy-start(s32[8,12]{1,0:T(8,128)} %param.11) | copy-start | bytes 1156
  21.6 14.0 %copy-start.8 = (s32[16]{0:T(128)S(1)}, s32[16]{0:T(128)}, u32[]{:S(2)}) copy-start(s32[16]{0:T(128)} %param.16) | copy-start | bytes 196
  21.6 14.1 %copy-start.9 = (s32[16,16]{1,0:T(8,128)S(1)}, s32[16,16]{1,0:T(8,128)}, u32[]{:S(2)}) copy-start(s32[16,16]{1,0:T(8,128)} %param.15) | copy-start | bytes 3076
  21.6 14.1 %copy-start.10 = (s32[16,16]{1,0:T(8,128)S(1)}, s32[16,16]{1,0:T(8,128)}, u32[]{:S(2)}) copy-start(s32[16,16]{1,0:T(8,128)} %param.14) | copy-start | bytes 3076
  23.4 30.0 %copy-start.11 = (s32[8]{0:T(128)S(1)}, s32[8]{0:T(128)}, u32[]{:S(2)}) copy-start(s32[8]{0:T(128)} %param.12) | copy-start | bytes 100
  24.3 19.4 %all-to-all-start = ((bf16[16,2,4,8,256]{4,3,2,1,0:T(8,128)(2,1)}), bf16[16,2,4,8,256]{4,3,2,1,0:T(8,128)(2,1)S(1)}, u32[]{:S(2)}, u32[]{:S(2)}) async-start(bf16[16,2,4,8,256]{4,3,2,1,0:T(8,128)(2,1)} %bitcast.34), calls=%async_computation | async-start | bytes 1048576 | tf_op jit(solution)/shard_map/all_to_all | solution.py:131
  43.8 18.9 %collective-permute-start.3 = (bf16[16,2,4,8,256]{4,3,2,1,0:T(8,128)(2,1)S(1)}, bf16[16,2,4,8,256]{4,3,2,1,0:T(8,128)(2,1)S(1)}, u32[]{:S(2)}, u32[]{:S(2)}) collective-permute-start(bf16[16,2,4,8,256]{4,3,2,1,0:T(8,128)(2,1)S(1)} %all-to-all-done), channel_id=1, source_target_pairs={{16,0},{32,16},{48,32},{64,48},{80,64},{96,80},{112,96},{128,112},... | collective-permute-start | bytes 1572872 | tf_op jit(solution)/shard_map/ppermute | solution.py:27
  51.0 18.1 %collective-permute-start.2 = (bf16[16,2,4,8,256]{4,3,2,1,0:T(8,128)(2,1)S(1)}, bf16[16,2,4,8,256]{4,3,2,1,0:T(8,128)(2,1)}, u32[]{:S(2)}, u32[]{:S(2)}) collective-permute-start(bf16[16,2,4,8,256]{4,3,2,1,0:T(8,128)(2,1)S(1)} %all-to-all-done), channel_id=1, source_target_pairs={{0,16},{16,32},{32,48},{48,64},{64,80},{80,96},{96,112},{112,128},... | collective-permute-start | bytes 1572872 | tf_op jit(solution)/shard_map/ppermute | solution.py:24
  73.1 48.6 %all-to-all-start.1 = ((bf16[16,2,4,8,256]{4,3,2,1,0:T(8,128)(2,1)}), bf16[16,2,4,8,256]{4,3,2,1,0:T(8,128)(2,1)}, u32[]{:S(2)}, u32[]{:S(2)}) async-start(bf16[16,2,4,8,256]{4,3,2,1,0:T(8,128)(2,1)} %pad_maximum_fusion.2), calls=%async_computation.1 | async-start | bytes 1048576 | tf_op jit(solution)/shard_map/all_to_all | solution.py:163
  80.2 1.0 copy-start.5
  90.0 23.5 %slice-start = ((s8[6291456]{0:T(1024)(128)(4,1)}), s8[2097152]{0:T(1024)(128)(4,1)S(1)}, s32[]{:S(2)}) async-start(s8[6291456]{0:T(1024)(128)(4,1)} %bitcast.235), calls=%async_computation.2 | async-start | bytes 4194304
  106.9 6.6 %slice-start.1 = ((s8[6291456]{0:T(1024)(128)(4,1)}), s8[4194304]{0:T(1024)(128)(4,1)S(1)}, s32[]{:S(2)}) async-start(s8[6291456]{0:T(1024)(128)(4,1)} %bitcast.235), calls=%async_computation.3 | async-start | bytes 8388608
  129.4 5.0 %copy-start.4 = (bf16[8,2,128,128]{3,2,1,0:T(8,128)(2,1)S(1)}, bf16[8,2,128,128]{3,2,1,0:T(8,128)(2,1)}, u32[]{:S(2)}) copy-start(bf16[8,2,128,128]{3,2,1,0:T(8,128)(2,1)} %param.13) | copy-start | bytes 1572868
  134.7 1.2 copy-start.6
  135.4 2.6 %copy-start.1 = (bf16[316,2,4,8]{0,3,2,1:T(8,128)(2,1)S(1)}, bf16[316,2,4,8]{0,3,2,1:T(8,128)(2,1)}, u32[]{:S(2)}) copy-start(bf16[316,2,4,8]{0,3,2,1:T(8,128)(2,1)} %param.17) | copy-start | bytes 121348
where the time goes:
time: 139 us; the launch traced here: 138 us
  matrix products  34.8 us (25%)
  starting transfers between devices  33.3 us (24%)
  local copies, waits for them, and re-layouts  30 us (22%)
  waiting for transfers between devices  23.2 us (17%)
  other arithmetic  16.2 us (12%)
    gather x2, local copies, waits for them, and re-layouts, per_device(): picked = widened[local_ids]  23.7 us
    all_to_all x1, starting transfers between devices, per_device(): lax.all_to_all(spread, ('theta', 'phi'), split_axis=0, concat_axis=0, til...  11.1 us
    ppermute x2, starting transfers between devices, padded(): lax.ppermute(lax.slice_in_dim(block, 0, width, axis=dim), axis, backward)  9.75 us
    ppermute x2, waiting for transfers between devices, padded(): lax.ppermute(lax.slice_in_dim(block, 0, width, axis=dim), axis, backward)  9.23 us
    dot_general x1, matrix products, per_device(): jnp.einsum('vl,bculr->bcuvr', full_phi, partial_up, precision=highest)  9.16 us
    all_to_all x1, waiting for transfers between devices, per_device(): lax.all_to_all(spread, ('theta', 'phi'), split_axis=0, concat_axis=0, til...  7.64 us
    all_to_all x1, starting transfers between devices, per_device(): lax.all_to_all(incoming, ('theta', 'phi'), split_axis=0, concat_axis=0, t...  7.11 us
    select_n x1, other arithmetic, per_device(): jnp.where(in_use[:, :, None, None, None], picked, jnp.zeros((), picked.dt...  6.58 us
  transfers between devices with their start and end apart: 6, of which 3 were waited for; matrix products, arithmetic and copies ran while one was open for 46% of the time, Pallas kernels for 0%

commit v1 on v0

v1 whole, which is shorter than its diff:
```python
import functools
import math

import jax
import jax.numpy as jnp
import numpy as np
from jax import lax
from jax.experimental import pallas as pl
from jax.experimental.pallas import tpu as pltpu
from jax.sharding import PartitionSpec as P

MESH = pl.DeviceIdType.MESH
BF = jnp.bfloat16
F32 = jnp.float32

TL, PL, TU, PU = 8, 16, 16, 32
WEIGHT_UP = (-0.0546875, 0.8203125, 0.2734375, -0.0390625)
WEIGHT_DOWN = (-0.0390625, 0.2734375, 0.8203125, -0.0546875)
PHASE_SCALE = 1.3
EARLY = 2
MIDDLE = 4


def lagrange(rows, cols, wrap):
    out = np.zeros((rows, cols), np.float64)
    for u in range(rows):
        i, e = u // 2, u % 2
        for k in range(4):
            node = i + e - 2 + k
            node = node % cols if wrap else min(max(node, 0), cols - 1)
            out[u, node] += (WEIGHT_UP if e == 1 else WEIGHT_DOWN)[k]
    return out


def tables():
    theta, phi = lagrange(TU, TL, False), lagrange(PU, PL, True)
    full = np.einsum("ut,vl->uvtl", theta, phi).reshape(TU, PU, TL * PL)
    a = (math.pi * (np.arange(TU) + 0.5) / TU)[:, None]
    c = (2.0 * math.pi * (np.arange(PU) + 0.5) / PU)[None, :]
    angle = []
    for o in range(4):
        sx, sy, sz = 2 * (o % 2) - 1, 2 * (o // 2 % 2) - 1, 2 * (o // 4) - 1
        angle.append(
            PHASE_SCALE
            * (sx * np.sin(a) * np.cos(c) + sy * np.sin(a) * np.sin(c) + sz * np.cos(a) * np.ones_like(c))
        )
    angle = np.stack(angle, -1)

    def banded(x):
        x = x.reshape(4, 4, 4, 8, -1).transpose(0, 2, 1, 3, 4)
        return x.reshape(512, -1)

    interp, angle = banded(full), banded(angle)
    phase = np.stack([np.cos(angle), np.sin(angle)], -1).reshape(512, 8)
    return interp.astype(np.float32), phase.astype(np.float32)


def split(x):
    high = x.astype(BF)
    return high, (x - high.astype(F32)).astype(BF)


def dot(a, b):
    return jnp.dot(a, b, preferred_element_type=F32)


def stacked(re, im):
    return jnp.concatenate(
        [jnp.concatenate([re, -im], axis=1), jnp.concatenate([im, re], axis=1)], axis=0
    )


def kernel(
    ids_ref, count_ref, x_hbm, blocks_hbm, rad_ref, part_ref, vec_ref, table_ref, interp_ref, phase_ref,
    interp_t_ref, phase_t_ref, out_hbm,
    xb, blocks, w_hi, w_lo, wt, gain, spread, mine, halo, coup, tb, acc, back, returned, rad_t, out,
    x_send, x_recv, a_send, a_recv, h_send, h_recv, b_send, b_recv, local_sem,
):
    box, th, ph = lax.axis_index("box"), lax.axis_index("theta"), lax.axis_index("phi")
    rank = box * 16 + th * 4 + ph
    mine_id = th * 4 + ph

    def ranked(r):
        r = lax.rem(r + 256, 256)
        return {"box": r // 16, "theta": lax.rem(r // 4, 4), "phi": lax.rem(r, 4)}

    def flipped(kb):
        hi, lo = th // 2, lax.rem(th, 2)
        hi = hi + (kb // 2) * (1 - 2 * hi)
        lo = lo + (kb % 2) * (1 - 2 * lo)
        return hi * 2 + lo

    above = {"box": lax.rem(box + 1, 16)}
    below = {"box": lax.rem(box + 15, 16)}

    own_x = pltpu.make_async_copy(x_hbm, xb.at[pl.ds(8, 8)], local_sem.at[0])
    own_x.start()
    own_blocks = pltpu.make_async_copy(blocks_hbm, blocks, local_sem.at[1])
    own_blocks.start()

    barrier = pltpu.get_barrier_semaphore()
    for device in (ranked(rank + 1), ranked(rank - 1), above, below):
        pl.semaphore_signal(barrier, inc=1, device_id=device, device_id_type=MESH)
    for k in range(1, 16):
        device = {"theta": flipped(k // 4), "phi": lax.rem(ph + k % 4, 4)}
        pl.semaphore_signal(barrier, inc=1, device_id=device, device_id_type=MESH)

    for q in range(4):
        for part in range(2):
            cols = pl.ds((2 * q + part) * 128, 128)
            high, low = split(phase_ref[:, 2 * q + part : 2 * q + part + 1] * interp_ref[...])
            w_hi[:, cols] = high
            w_lo[:, cols] = low
    xb[24] = jnp.zeros((256, 256), BF)
    own_x.wait()
    pl.semaphore_wait(barrier, 19)

    def shift(i, way):
        return pltpu.make_async_remote_copy(
            src_ref=xb.at[8 + i],
            dst_ref=xb.at[i if way == 0 else 16 + i],
            send_sem=x_send.at[way, i],
            recv_sem=x_recv.at[way, i],
            device_id=ranked(rank + 1) if way == 0 else ranked(rank - 1),
            device_id_type=MESH,
        )

    def exchange(src, dst, send, recv, kb, kp):
        target_th, target_ph = flipped(kb), lax.rem(ph + kp, 4)
        k = kb * 4 + kp
        return pltpu.make_async_remote_copy(
            src_ref=src.at[target_th * 4 + target_ph],
            dst_ref=dst.at[mine_id],
            send_sem=send.at[k],
            recv_sem=recv.at[k],
            device_id={"theta": target_th, "phi": target_ph},
            device_id_type=MESH,
        )

    def pass_on(k, source, way):
        return pltpu.make_async_remote_copy(
            src_ref=mine.at[source],
            dst_ref=halo.at[way, source],
            send_sem=h_send.at[way, k],
            recv_sem=h_recv.at[way, k],
            device_id=above if way == 0 else below,
            device_id_type=MESH,
        )

    for i in range(EARLY):
        for way in range(2):
            shift(i, way).start()

    for q in range(4):
        low_o = dot(stacked(rad_ref[q, 0], rad_ref[q, 1]), xb[8 + q]).astype(BF).astype(F32)
        high_o = dot(stacked(rad_ref[7 - q, 0], rad_ref[7 - q, 1]), xb[15 - q]).astype(BF).astype(F32)
        total, diff = low_o + high_o, low_o - high_o
        rows, rows2 = pl.ds(q * 256, 128), pl.ds(q * 256 + 128, 128)
        for c, first, second in ((0, total[:128], -diff[128:]), (1, total[128:], diff[:128])):
            high, low = split(first)
            gain[c, rows] = high
            gain[2 + c, rows] = low
            high, low = split(second)
            gain[c, rows2] = high
            gain[2 + c, rows2] = low

    for kb in (3, 2, 1, 0):
        target = flipped(kb)
        rows = pl.ds(pl.multiple_of(target * 128, 128), 128)
        high, low = w_hi[rows], w_lo[rows]
        for c in range(2):
            piece = dot(high, gain[c]) + dot(high, gain[2 + c]) + dot(low, gain[c])
            spread[pl.ds(target * 4, 4), c * 32 : c * 32 + 32] = piece.astype(BF).reshape(4, 32, 256)
        for kp in (2, 1, 3, 0):
            if kb or kp:
                exchange(spread, mine, a_send, a_recv, kb, kp).start()
    mine[mine_id] = spread[mine_id]
    for way in range(2):
        pass_on(0, mine_id, way).start()
    for i in range(EARLY, EARLY + MIDDLE):
        for way in range(2):
            shift(i, way).start()

    hot = (lax.broadcasted_iota(jnp.int32, (316, 256), 0) == vec_ref[...]).astype(F32).astype(BF)
    chosen = dot(table_ref[...], hot).astype(BF)
    lane = lax.broadcasted_iota(jnp.int32, (256, 128), 1)
    row = lax.broadcasted_iota(jnp.int32, (256, 128), 0)
    match = lax.rem(lane, 64) == part_ref[...]
    left = lax.broadcasted_iota(jnp.int32, (32, 128), 1) < 64
    for d in range(16):
        picked = jnp.where(match & (row // 16 == d), 1.0, 0.0).astype(BF)
        both = dot(chosen, picked)
        re, im = both[:32], both[32:]
        coup[64 * d : 64 * d + 32] = jnp.where(left, re, -im).astype(BF)
        coup[64 * d + 32 : 64 * d + 64] = jnp.where(left, im, re).astype(BF)

    def spread_out(n):
        at = lax.broadcasted_iota(jnp.int32, (128, 256), 0)
        to = lax.broadcasted_iota(jnp.int32, (128, 256), 1)
        same = (at // 64 == lax.rem(to // 32, 2)) & (lax.rem(at, 64) == 4 * n + to // 64)
        grow = jnp.where(same, 1.0, 0.0).astype(BF)
        s_row = lax.rem(lax.broadcasted_iota(jnp.int32, (256, 256), 0), 32)
        s_col = lax.rem(lax.broadcasted_iota(jnp.int32, (256, 256), 1), 32)
        for m in range(4):
            wide = dot(coup[256 * m : 256 * m + 256], grow)
            tb[n, 256 * m : 256 * m + 256] = jnp.where(s_row == s_col, wide, 0.0).astype(BF)

    def source_of(kb, kp):
        return flipped(kb) * 4 + lax.rem(ph + 4 - kp, 4)

    def relay(k):
        kb, kp = k // 4, lax.rem(k, 4)
        source = source_of(kb, kp)
        pltpu.make_async_remote_copy(
            src_ref=spread.at[0],
            dst_ref=mine.at[source],
            send_sem=a_send.at[k],
            recv_sem=a_recv.at[k],
            device_id=above,
            device_id_type=MESH,
        ).wait_recv()
        for way in range(2):
            pass_on(k, source, way).start()

    def first(i, carry):
        relay(7 - i)
        spread_out(i)
        return carry

    def second(i, carry):
        relay(15 - i)

        @pl.when(i < 5)
        def _():
            spread_out(7 + i)

        return carry

    lax.fori_loop(0, 7, first, 0)
    lax.fori_loop(0, 8, second, 0)

    for m in range(4):
        rows = slice(256 * m, 256 * m + 256)
        total = dot(tb[4, rows], mine[0:4].reshape(256, 256))
        for n in range(1, 4):
            total = total + dot(tb[4 + n, rows], mine[4 * n : 4 * n + 4].reshape(256, 256))
        acc[rows] = total

    for q in range(4):
        for part in range(2):
            rows = pl.ds((2 * q + part) * 128, 128)
            high, low = split(phase_t_ref[2 * q + part : 2 * q + part + 1, :] * interp_t_ref[...])
            wt[rows, 0:512] = high
            wt[rows, 512:1024] = low
    for o in range(8):
        re, im = rad_ref[o, 0].astype(F32).T.astype(BF), rad_ref[o, 1].astype(F32).T.astype(BF)
        rad_t[o] = stacked(re, -im)

    def arrived(kb):
        for kp in range(4):
            for way in range(2):
                pass_on(kb * 4 + kp, source_of(kb, kp), way).wait_recv()

    def halo_term(kb, rows):
        n = flipped(kb)
        low = dot(tb[n, rows], halo[0, pl.ds(n * 4, 4)].reshape(256, 256))
        high = dot(tb[8 + n, rows], halo[1, pl.ds(n * 4, 4)].reshape(256, 256))
        return low + high

    for kb in (1, 0, 3):
        arrived(kb)
        for m in range(4):
            rows = slice(256 * m, 256 * m + 256)
            acc[rows] += halo_term(kb, rows)
    arrived(2)
    for kb in (3, 2, 1, 0):
        target = flipped(kb)
        rows = pl.ds(pl.multiple_of(target * 256, 256), 256)
        total = acc[rows] + halo_term(2, rows)
        back[pl.ds(target * 4, 4)] = total.astype(BF).reshape(4, 64, 256)
        for kp in (2, 1, 3, 0):
            if kb or kp:
                exchange(back, returned, b_send, b_recv, kb, kp).start()
    returned[mine_id] = back[mine_id]
    for i in range(EARLY + MIDDLE, 8):
        for way in range(2):
            shift(i, way).start()

    for i in range(8):
        for way in range(2):
            shift(i, way).wait_recv()
    own_blocks.wait()

    def near(b, carry):
        left_all, right_all = [], []
        for j in range(12):
            at = jnp.where(j < count_ref[b], ids_ref[b, j] - (rank * 8 - 8), 24)
            left_all.append(stacked(blocks[b, j, 0], blocks[b, j, 1]))
            right_all.append(xb[jnp.clip(at, 0, 24)])
        total = dot(left_all[0], right_all[0])
        for j in range(1, 12):
            total = total + dot(left_all[j], right_all[j])
        out[b] = total
        return carry

    lax.fori_loop(0, 8, near, 0)

    for k in range(1, 16):
        pltpu.make_async_remote_copy(
            src_ref=back.at[0],
            dst_ref=returned.at[source_of(k // 4, k % 4)],
            send_sem=b_send.at[k],
            recv_sem=b_recv.at[k],
            device_id=above,
            device_id_type=MESH,
        ).wait_recv()

    def result(o):
        return pltpu.make_async_copy(out.at[o], out_hbm.at[o], local_sem.at[2 + o])

    field_re = returned[:, 0:32].reshape(512, 256)
    field_im = returned[:, 32:64].reshape(512, 256)
    for q in range(4):
        rows = slice(256 * q, 256 * q + 256)
        re = dot(wt[rows, 0:512], field_re) + dot(wt[rows, 512:1024], field_re)
        im = dot(wt[rows, 0:512], field_im) + dot(wt[rows, 512:1024], field_im)
        cr, sr, ci, si = re[:128], re[128:], im[:128], im[128:]
        leaf = jnp.concatenate([cr + si, ci - sr], axis=0).astype(BF)
        out[q] += dot(rad_t[q], leaf)
        result(q).start()
        leaf = jnp.concatenate([cr - si, ci + sr], axis=0).astype(BF)
        out[7 - q] += dot(rad_t[7 - q], leaf)
        result(7 - q).start()

    for i in range(8):
        for way in range(2):
            shift(i, way).wait_send()
    for k in range(1, 16):
        exchange(spread, mine, a_send, a_recv, k // 4, k % 4).wait_send()
        exchange(back, returned, b_send, b_recv, k // 4, k % 4).wait_send()
    for k in range(16):
        for way in range(2):
            pass_on(k, source_of(k // 4, k % 4), way).wait_send()
    for o in range(8):
        result(o).wait()


def per_device(coeffs, near_blocks, near_ids, near_count, radiation, partners, vector_ids, pair_count, translation):
    interp, phase = tables()
    group = lax.axis_index("box")
    used = jnp.arange(16)[None, :] < pair_count[:, None]
    part = jnp.where(used, partners - (group * 16 - 16), -1).reshape(256, 1)
    vec = vector_ids.reshape(1, 256)
    table = translation.transpose(1, 2, 3, 0).reshape(64, 316)
    vmem, any_, smem = (pl.BlockSpec(memory_space=s) for s in (pltpu.VMEM, pl.ANY, pltpu.SMEM))
    dma = pltpu.SemaphoreType.DMA
    product = pl.pallas_call(
        kernel,
        out_shape=jax.ShapeDtypeStruct((8, 256, 256), F32),
        in_specs=[smem, smem, any_, any_, vmem, vmem, vmem, vmem, vmem, vmem, vmem, vmem],
        out_specs=any_,
        scratch_shapes=[
            pltpu.VMEM((25, 256, 256), BF),
            pltpu.VMEM((8, 12, 2, 128, 128), BF),
            pltpu.VMEM((512, 1024), BF),
            pltpu.VMEM((512, 1024), BF),
            pltpu.VMEM((1024, 1024), BF),
            pltpu.VMEM((4, 1024, 256), BF),
            pltpu.VMEM((16, 64, 256), BF),
            pltpu.VMEM((16, 64, 256), BF),
            pltpu.VMEM((2, 16, 64, 256), BF),
            pltpu.VMEM((1024, 128), BF),
            pltpu.VMEM((12, 1024, 256), BF),
            pltpu.VMEM((1024, 256), F32),
            pltpu.VMEM((16, 64, 256), BF),
            pltpu.VMEM((16, 64, 256), BF),
            pltpu.VMEM((8, 256, 256), BF),
            pltpu.VMEM((8, 256, 256), F32),
            dma((2, 8)),
            dma((2, 8)),
            dma((16,)),
            dma((16,)),
            dma((2, 16)),
            dma((2, 16)),
            dma((16,)),
            dma((16,)),
            dma((10,)),
        ],
        compiler_params=pltpu.CompilerParams(
            collective_id=0, has_side_effects=True, vmem_limit_bytes=56 * 1024 * 1024
        ),
    )(
        near_ids,
        near_count,
        coeffs.reshape(8, 256, 256),
        near_blocks,
        radiation,
        part,
        vec,
        table,
        jnp.asarray(interp),
        jnp.asarray(phase),
        jnp.asarray(np.ascontiguousarray(interp.T)),
        jnp.asarray(np.ascontiguousarray(phase.T)),
    )
    return product.reshape(8, 2, 128, 256)


def solution(mesh):
    ranks = ("box", "theta", "phi")
    in_specs = (
        P(ranks, None, None, None),
        P(ranks, None, None, None, None),
        P(ranks, None),
        P(ranks),
        P(ranks, None, None, None),
        P("box", None),
        P("box", None),
        P("box"),
        P(None, None, "theta", "phi"),
    )
    return jax.shard_map(
        per_device, mesh=mesh, in_specs=in_specs, out_specs=P(ranks, None, None, None), check_vma=False
    )
```

time: 139 us -> 72.5 us (0.52)
  the two profiles are of different devices: /device:TPU:26 before, /device:TPU:12 now
where the time goes in v1:
time: 72.5 us; the launch traced here: 72.2 us
  Pallas kernels  66.2 us (91%)
  local copies, waits for them, and re-layouts  5.23 us (7%)
  other arithmetic  0.77 us (1%)
    pallas_call x1, Pallas kernels, per_device(): pl.pallas_call(kernel, out_shape=jax.ShapeDtypeStruct((8, 256, 256), F32)...  66.2 us
    unnamed x1, local copies, waits for them, and re-layouts  3.1 us

profile of v1, /device:TPU:12, one launch (start us, length us, event | category | flops | bytes accessed | tf_op | source)
XLA Modules:
  0.0 72.2 jit_solution(811575818925459387)
XLA Ops:
  0.0 1.4 %reshape.18.vec_ref = s32[1,256]{1,0:T(1,128)} reshape(s32[16,16]{1,0:T(8,128)} %param.19) | data formatting | bytes 2048 | tf_op jit(solution)/shard_map/reshape | solution.py:353
  1.4 0.8 %subtract_select_fusion = s32[16,16]{1,0:T(8,128)S(1)} fusion(s32[16,16]{1,0:T(8,128)} %param.18, s32[]{:T(128)S(6)} %sub.9, s32[16]{0:T(128)} %param.20), kind=kLoop, calls=%fused_computation | loop fusion | flops 768 | bytes 2116 | tf_op jit(solution)/shard_map/jit(_where)/select_n | solution.py:352
  2.1 0.8 %reshape.21.part_ref = s32[256,1]{1,0:T(8,128)} reshape(s32[16,16]{1,0:T(8,128)S(1)} %subtract_select_fusion) | data formatting | bytes 2048 | tf_op jit(solution)/shard_map/reshape | solution.py:352
  2.9 66.2 %shard_map.127 = f32[8,256,256]{2,1,0:T(8,128)} custom-call(s32[8,12]{1,0:T(8,128)} %ids_ref.1, s32[8]{0:T(128)} %count_ref.1, bf16[8,256,256]{2,1,0:T(8,128)(2,1)} %bitcast.6, bf16[8,12,2,128,128]{4,3,2,1,0:T(8,128)(2,1)} %blocks_hbm.1, bf16[8,2,128,128]{3,2,1,0:T(8,128)(2,1)} %rad_ref.1, s32[256,1]{1,0:T(8,128)} %reshape.21.part_ref, ...), custom_call_target="tpu_custom_call" | custom-call | tf_op jit(solution)/shard_map/pallas_call | solution.py:357
  69.1 3.1 %copy.16 = f32[8,2,128,256]{3,2,1,0:T(8,128)} copy(f32[8,2,128,256]{3,2,1,0:T(8,128)} %bitcast.5) | data formatting | bytes 4194304

commit v2 on v1

--- a/solution.py
+++ b/solution.py
@@ -17,8 +17,10 @@
 WEIGHT_UP = (-0.0546875, 0.8203125, 0.2734375, -0.0390625)
 WEIGHT_DOWN = (-0.0390625, 0.2734375, 0.8203125, -0.0546875)
 PHASE_SCALE = 1.3
-EARLY = 2
-MIDDLE = 4
+EARLY = 1
+MIDDLE = 5
+RELAY = True
+LIMIT = 56
 
 
 def lagrange(rows, cols, wrap):
@@ -71,9 +73,10 @@
 
 
 def kernel(
-    ids_ref, count_ref, x_hbm, blocks_hbm, rad_ref, part_ref, vec_ref, table_ref, interp_ref, phase_ref,
-    interp_t_ref, phase_t_ref, out_hbm,
-    xb, blocks, w_hi, w_lo, wt, gain, spread, mine, halo, coup, tb, acc, back, returned, rad_t, out,
+    ids_ref, count_ref, used_ref, x_hbm, blocks_hbm, rad_hbm, part_ref, vec_ref, table_hbm, interp_hbm, phase_ref,
+    interp_t_hbm, phase_t_ref, out_hbm,
+    rad_ref, table_ref, interp_ref, interp_t_ref,
+    xb, arrived_x, blocks, w_hi, w_lo, wt, gain, spread, mine, halo, coup, tb, acc, back, returned, rad_t, out,
     x_send, x_recv, a_send, a_recv, h_send, h_recv, b_send, b_recv, local_sem,
 ):
     box, th, ph = lax.axis_index("box"), lax.axis_index("theta"), lax.axis_index("phi")
@@ -90,35 +93,66 @@
         lo = lo + (kb % 2) * (1 - 2 * lo)
         return hi * 2 + lo
 
+    def source_of(kb, kp):
+        return flipped(kb) * 4 + lax.rem(ph + 4 - kp, 4)
+
     above = {"box": lax.rem(box + 1, 16)}
     below = {"box": lax.rem(box + 15, 16)}
 
-    own_x = pltpu.make_async_copy(x_hbm, xb.at[pl.ds(8, 8)], local_sem.at[0])
-    own_x.start()
-    own_blocks = pltpu.make_async_copy(blocks_hbm, blocks, local_sem.at[1])
-    own_blocks.start()
+    has_above, has_below = box < 15, box > 0
+    has_next, has_last = rank < 255, rank > 0
+    toward = (has_above, has_below)
+    beside = (has_next, has_last)
+    corner = RELAY & ((lax.rem(box, 8) == 0) | (lax.rem(box, 8) == 7))
+
+    for way in range(2):
+
+        @pl.when(jnp.logical_not(toward[1 - way]))
+        def _():
+            halo[way] = jnp.zeros((16, 64, 256), BF)
+
+        @pl.when(jnp.logical_not(beside[1 - way]))
+        def _():
+            arrived_x[way] = jnp.zeros((8, 256, 256), BF)
 
     barrier = pltpu.get_barrier_semaphore()
-    for device in (ranked(rank + 1), ranked(rank - 1), above, below):
+
+    def greet(device):
         pl.semaphore_signal(barrier, inc=1, device_id=device, device_id_type=MESH)
+
+    for flag, device in (
+        (has_next, ranked(rank + 1)),
+        (has_last, ranked(rank - 1)),
+        (has_above, above),
+        (has_below, below),
+    ):
+        pl.when(flag)(functools.partial(greet, device))
+    for flag, device in (
+        (corner, {"box": lax.rem(box + 8, 16)}),
+        (corner, {"box": box // 8 * 8 + 7 - lax.rem(box, 8)}),
+    ):
+        pl.when(flag)(functools.partial(greet, device))
     for k in range(1, 16):
-        device = {"theta": flipped(k // 4), "phi": lax.rem(ph + k % 4, 4)}
-        pl.semaphore_signal(barrier, inc=1, device_id=device, device_id_type=MESH)
-
-    for q in range(4):
-        for part in range(2):
-            cols = pl.ds((2 * q + part) * 128, 128)
-            high, low = split(phase_ref[:, 2 * q + part : 2 * q + part + 1] * interp_ref[...])
-            w_hi[:, cols] = high
-            w_lo[:, cols] = low
+        greet({"theta": flipped(k // 4), "phi": lax.rem(ph + k % 4, 4)})
+
+    def load(n, src, dst):
+        copy = pltpu.make_async_copy(src, dst, local_sem.at[n])
+        copy.start()
+        return copy
+
+    own_rad = load(0, rad_hbm, rad_ref)
+    own_x = load(1, x_hbm, xb.at[pl.ds(8, 8)])
+    own_interp = load(2, interp_hbm, interp_ref)
+    own_table = load(3, table_hbm, table_ref)
+    own_interp_t = load(4, interp_t_hbm, interp_t_ref)
+    own_blocks = load(5, blocks_hbm, blocks)
+
     xb[24] = jnp.zeros((256, 256), BF)
-    own_x.wait()
-    pl.semaphore_wait(barrier, 19)
-
-    def shift(i, way):
+    def shift(n, way):
+        i = 7 - n if way == 0 else n
         return pltpu.make_async_remote_copy(
             src_ref=xb.at[8 + i],
-            dst_ref=xb.at[i if way == 0 else 16 + i],
+            dst_ref=arrived_x.at[way, i],
             send_sem=x_send.at[way, i],
             recv_sem=x_recv.at[way, i],
             device_id=ranked(rank + 1) if way == 0 else ranked(rank - 1),
@@ -137,7 +171,24 @@
             device_id_type=MESH,
         )
 
+    def detoured(k, way):
+        at = 7 if way == 0 else 8
+        return RELAY & (box == at) & (lax.rem(k, 2) == 1)
+
     def pass_on(k, source, way):
+        off = jnp.where(detoured(k, way), 1, 0)
+        slot = way + off * (1 - 2 * way)
+        next_box = lax.rem(box + (1 if way == 0 else 15), 16)
+        return pltpu.make_async_remote_copy(
+            src_ref=mine.at[source],
+            dst_ref=halo.at[slot, source],
+            send_sem=h_send.at[way, k],
+            recv_sem=h_recv.at[slot, k],
+            device_id={"box": next_box + off * ((15 if way == 0 else 0) - next_box)},
+            device_id_type=MESH,
+        )
+
+    def landed(k, source, way):
         return pltpu.make_async_remote_copy(
             src_ref=mine.at[source],
             dst_ref=halo.at[way, source],
@@ -147,10 +198,27 @@
             device_id_type=MESH,
         )
 
-    for i in range(EARLY):
-        for way in range(2):
-            shift(i, way).start()
-
+    def hand_over(k, source, way):
+        return pltpu.make_async_remote_copy(
+            src_ref=halo.at[1 - way, source],
+            dst_ref=halo.at[way, source],
+            send_sem=h_send.at[way, k],
+            recv_sem=h_recv.at[way, k],
+            device_id={"box": 8 if way == 0 else 7},
+            device_id_type=MESH,
+        )
+
+    def detour(k):
+        for way in range(2):
+
+            @pl.when(box == (15 if way == 0 else 0))
+            def _():
+                source = source_of(k // 4, lax.rem(k, 4))
+                landed(k, source, 1 - way).wait_recv()
+                hand_over(k, source, way).start()
+
+    own_rad.wait()
+    own_x.wait()
     for q in range(4):
         low_o = dot(stacked(rad_ref[q, 0], rad_ref[q, 1]), xb[8 + q]).astype(BF).astype(F32)
         high_o = dot(stacked(rad_ref[7 - q, 0], rad_ref[7 - q, 1]), xb[15 - q]).astype(BF).astype(F32)
@@ -164,6 +232,20 @@
             gain[c, rows2] = high
             gain[2 + c, rows2] = low
 
+    flags = [jnp.where(flag, 1, 0) for flag in toward + beside + (corner, corner)]
+    pl.semaphore_wait(barrier, 15 + sum(flags))
+
+    for i in range(EARLY):
+        for way in range(2):
+            pl.when(beside[way])(shift(i, way).start)
+
+    own_interp.wait()
+    for q in range(4):
+        for part in range(2):
+            cols = pl.ds((2 * q + part) * 128, 128)
+            high, low = split(phase_ref[:, 2 * q + part : 2 * q + part + 1] * interp_ref[...])
+            w_hi[:, cols] = high
+            w_lo[:, cols] = low
     for kb in (3, 2, 1, 0):
         target = flipped(kb)
         rows = pl.ds(pl.multiple_of(target * 128, 128), 128)
@@ -176,20 +258,27 @@
                 exchange(spread, mine, a_send, a_recv, kb, kp).start()
     mine[mine_id] = spread[mine_id]
     for way in range(2):
-        pass_on(0, mine_id, way).start()
+        pl.when(toward[way])(pass_on(0, mine_id, way).start)
     for i in range(EARLY, EARLY + MIDDLE):
         for way in range(2):
-            shift(i, way).start()
-
-    hot = (lax.broadcasted_iota(jnp.int32, (316, 256), 0) == vec_ref[...]).astype(F32).astype(BF)
+            pl.when(beside[way])(shift(i, way).start)
+
+    slot = lax.broadcasted_iota(jnp.int32, (1, 16), 1)
+    first_source = box * 16 - 16
+    vec = jnp.concatenate([vec_ref[d : d + 1] for d in range(16)], axis=1)
+    part = jnp.concatenate(
+        [jnp.where(slot < used_ref[d], part_ref[d : d + 1] - first_source, -1) for d in range(16)], axis=1
+    )
+    hot = (lax.broadcasted_iota(jnp.int32, (316, 256), 0) == vec).astype(F32).astype(BF)
+    own_table.wait()
     chosen = dot(table_ref[...], hot).astype(BF)
-    lane = lax.broadcasted_iota(jnp.int32, (256, 128), 1)
-    row = lax.broadcasted_iota(jnp.int32, (256, 128), 0)
-    match = lax.rem(lane, 64) == part_ref[...]
+    row = lax.broadcasted_iota(jnp.int32, (128, 256), 0)
+    lane = lax.broadcasted_iota(jnp.int32, (128, 256), 1)
+    match = lax.rem(row, 64) == part
     left = lax.broadcasted_iota(jnp.int32, (32, 128), 1) < 64
     for d in range(16):
-        picked = jnp.where(match & (row // 16 == d), 1.0, 0.0).astype(BF)
-        both = dot(chosen, picked)
+        picked = jnp.where(match & (lane // 16 == d), 1.0, 0.0).astype(BF)
+        both = lax.dot_general(chosen, picked, (((1,), (1,)), ((), ())), preferred_element_type=F32)
         re, im = both[:32], both[32:]
         coup[64 * d : 64 * d + 32] = jnp.where(left, re, -im).astype(BF)
         coup[64 * d + 32 : 64 * d + 64] = jnp.where(left, im, re).astype(BF)
@@ -205,9 +294,6 @@
             wide = dot(coup[256 * m : 256 * m + 256], grow)
             tb[n, 256 * m : 256 * m + 256] = jnp.where(s_row == s_col, wide, 0.0).astype(BF)
 
-    def source_of(kb, kp):
-        return flipped(kb) * 4 + lax.rem(ph + 4 - kp, 4)
-
     def relay(k):
         kb, kp = k // 4, lax.rem(k, 4)
         source = source_of(kb, kp)
@@ -220,7 +306,7 @@
             device_id_type=MESH,
         ).wait_recv()
         for way in range(2):
-            pass_on(k, source, way).start()
+            pl.when(toward[way])(pass_on(k, source, way).start)
 
     def first(i, carry):
         relay(7 - i)
@@ -229,6 +315,8 @@
 
     def second(i, carry):
         relay(15 - i)
+        if RELAY:
+            detour(jnp.where(i < 4, 7 - 2 * i, 23 - 2 * i))
 
         @pl.when(i < 5)
         def _():
@@ -246,6 +334,7 @@
             total = total + dot(tb[4 + n, rows], mine[4 * n : 4 * n + 4].reshape(256, 256))
         acc[rows] = total
 
+    own_interp_t.wait()
     for q in range(4):
         for part in range(2):
             rows = pl.ds((2 * q + part) * 128, 128)
@@ -259,7 +348,7 @@
     def arrived(kb):
         for kp in range(4):
             for way in range(2):
-                pass_on(kb * 4 + kp, source_of(kb, kp), way).wait_recv()
+                pl.when(toward[1 - way])(landed(kb * 4 + kp, source_of(kb, kp), way).wait_recv)
 
     def halo_term(kb, rows):
         n = flipped(kb)
@@ -284,26 +373,38 @@
     returned[mine_id] = back[mine_id]
     for i in range(EARLY + MIDDLE, 8):
         for way in range(2):
-            shift(i, way).start()
-
-    for i in range(8):
-        for way in range(2):
-            shift(i, way).wait_recv()
+            pl.when(beside[way])(shift(i, way).start)
+
     own_blocks.wait()
 
-    def near(b, carry):
-        left_all, right_all = [], []
+    def collect(n):
+        for way in range(2):
+            i = 7 - n if way == 0 else n
+            pl.when(beside[1 - way])(shift(n, way).wait_recv)
+            xb[i + 16 * way] = arrived_x[way, i]
+
+    def near(b):
+        total = None
         for j in range(12):
             at = jnp.where(j < count_ref[b], ids_ref[b, j] - (rank * 8 - 8), 24)
-            left_all.append(stacked(blocks[b, j, 0], blocks[b, j, 1]))
-            right_all.append(xb[jnp.clip(at, 0, 24)])
-        total = dot(left_all[0], right_all[0])
-        for j in range(1, 12):
-            total = total + dot(left_all[j], right_all[j])
+            term = dot(stacked(blocks[b, j, 0], blocks[b, j, 1]), xb[jnp.clip(at, 0, 24)])
+            total = term if j == 0 else total + term
         out[b] = total
-        return carry
-
-    lax.fori_loop(0, 8, near, 0)
+
+    def near_pair(q):
+        if q == 3:
+            for n in range(4):
+                collect(n)
+        collect(7 - q)
+
+        def one(n, carry):
+            near(q + n * (7 - 2 * q))
+            return carry
+
+        lax.fori_loop(0, 2, one, 0)
+
+    for q in (3, 2):
+        near_pair(q)
 
     for k in range(1, 16):
         pltpu.make_async_remote_copy(
@@ -316,11 +417,13 @@
         ).wait_recv()
 
     def result(o):
-        return pltpu.make_async_copy(out.at[o], out_hbm.at[o], local_sem.at[2 + o])
+        return pltpu.make_async_copy(out.at[o], out_hbm.at[o], local_sem.at[6 + o])
 
     field_re = returned[:, 0:32].reshape(512, 256)
     field_im = returned[:, 32:64].reshape(512, 256)
-    for q in range(4):
+    for q in (3, 2, 1, 0):
+        if q < 2:
+            near_pair(q)
         rows = slice(256 * q, 256 * q + 256)
         re = dot(wt[rows, 0:512], field_re) + dot(wt[rows, 512:1024], field_re)
         im = dot(wt[rows, 0:512], field_im) + dot(wt[rows, 512:1024], field_im)
@@ -334,33 +437,36 @@
 
     for i in range(8):
         for way in range(2):
-            shift(i, way).wait_send()
+            pl.when(beside[way])(shift(i, way).wait_send)
     for k in range(1, 16):
         exchange(spread, mine, a_send, a_recv, k // 4, k % 4).wait_send()
         exchange(back, returned, b_send, b_recv, k // 4, k % 4).wait_send()
     for k in range(16):
         for way in range(2):
-            pass_on(k, source_of(k // 4, k % 4), way).wait_send()
+            pl.when(toward[way])(pass_on(k, source_of(k // 4, k % 4), way).wait_send)
+            if RELAY and k % 2:
+                pl.when(box == (15 if way == 0 else 0))(hand_over(k, source_of(k // 4, k % 4), way).wait_send)
     for o in range(8):
         result(o).wait()
 
 
 def per_device(coeffs, near_blocks, near_ids, near_count, radiation, partners, vector_ids, pair_count, translation):
     interp, phase = tables()
-    group = lax.axis_index("box")
-    used = jnp.arange(16)[None, :] < pair_count[:, None]
-    part = jnp.where(used, partners - (group * 16 - 16), -1).reshape(256, 1)
-    vec = vector_ids.reshape(1, 256)
     table = translation.transpose(1, 2, 3, 0).reshape(64, 316)
     vmem, any_, smem = (pl.BlockSpec(memory_space=s) for s in (pltpu.VMEM, pl.ANY, pltpu.SMEM))
     dma = pltpu.SemaphoreType.DMA
     product = pl.pallas_call(
         kernel,
         out_shape=jax.ShapeDtypeStruct((8, 256, 256), F32),
-        in_specs=[smem, smem, any_, any_, vmem, vmem, vmem, vmem, vmem, vmem, vmem, vmem],
+        in_specs=[smem, smem, smem, any_, any_, any_, vmem, vmem, any_, any_, vmem, any_, vmem],
         out_specs=any_,
         scratch_shapes=[
+            pltpu.VMEM((8, 2, 128, 128), BF),
+            pltpu.VMEM((64, 316), BF),
+            pltpu.VMEM((512, 128), F32),
+            pltpu.VMEM((128, 512), F32),
             pltpu.VMEM((25, 256, 256), BF),
+            pltpu.VMEM((2, 8, 256, 256), BF),
             pltpu.VMEM((8, 12, 2, 128, 128), BF),
             pltpu.VMEM((512, 1024), BF),
             pltpu.VMEM((512, 1024), BF),
@@ -384,19 +490,20 @@
             dma((2, 16)),
             dma((16,)),
             dma((16,)),
-            dma((10,)),
+            dma((14,)),
         ],
         compiler_params=pltpu.CompilerParams(
-            collective_id=0, has_side_effects=True, vmem_limit_bytes=56 * 1024 * 1024
+            collective_id=0, has_side_effects=True, vmem_limit_bytes=LIMIT * 1024 * 1024
         ),
     )(
         near_ids,
         near_count,
+        pair_count,
         coeffs.reshape(8, 256, 256),
         near_blocks,
         radiation,
-        part,
-        vec,
+        partners,
+        vector_ids,
         table,
         jnp.asarray(interp),
         jnp.asarray(phase),

time: 72.5 us -> 58.7 us (0.81)
  the two profiles are of different devices: /device:TPU:12 before, /device:TPU:26 now
where the time goes in v2:
time: 58.7 us; the launch traced here: 58.6 us
  Pallas kernels  55.5 us (95%)
  local copies, waits for them, and re-layouts  3.1 us (5%)
    pallas_call x1, Pallas kernels, per_device(): pl.pallas_call(kernel, out_shape=jax.ShapeDtypeStruct((8, 256, 256), F32)...  55.5 us
    unnamed x1, local copies, waits for them, and re-layouts  3.1 us

profile of v2, /device:TPU:26, one launch (start us, length us, event | category | flops | bytes accessed | tf_op | source)
XLA Modules:
  0.0 58.6 jit_solution(13367787134221749102)
XLA Ops:
  0.0 55.5 %shard_map.127 = f32[8,256,256]{2,1,0:T(8,128)} custom-call(s32[8,12]{1,0:T(8,128)} %ids_ref.1, s32[8]{0:T(128)} %count_ref.1, s32[16]{0:T(128)} %used_ref.1, bf16[8,256,256]{2,1,0:T(8,128)(2,1)} %bitcast.6, bf16[8,12,2,128,128]{4,3,2,1,0:T(8,128)(2,1)} %blocks_hbm.1, bf16[8,2,128,128]{3,2,1,0:T(8,128)(2,1)} %rad_hbm.1, s32[16,16]{1,0:T(8,128)} %part_ref.1, ...), custom_call_target="tpu_custom_call" | custom-call | tf_op jit(solution)/shard_map/pallas_call | solution.py:458
  55.5 3.1 %copy.15 = f32[8,2,128,256]{3,2,1,0:T(8,128)} copy(f32[8,2,128,256]{3,2,1,0:T(8,128)} %bitcast.5) | data formatting | bytes 4194304

commit v3 on v2

--- a/solution.py
+++ b/solution.py
@@ -18,9 +18,9 @@
 WEIGHT_DOWN = (-0.0390625, 0.2734375, 0.8203125, -0.0546875)
 PHASE_SCALE = 1.3
 EARLY = 1
-MIDDLE = 5
+MIDDLE = 6
 RELAY = True
-LIMIT = 56
+LIMIT = 40
 
 
 def lagrange(rows, cols, wrap):
@@ -74,9 +74,9 @@
 
 def kernel(
     ids_ref, count_ref, used_ref, x_hbm, blocks_hbm, rad_hbm, part_ref, vec_ref, table_hbm, interp_hbm, phase_ref,
-    interp_t_hbm, phase_t_ref, out_hbm,
+    interp_t_hbm, phase_t_ref, out,
     rad_ref, table_ref, interp_ref, interp_t_ref,
-    xb, arrived_x, blocks, w_hi, w_lo, wt, gain, spread, mine, halo, coup, tb, acc, back, returned, rad_t, out,
+    xb, arrived_x, blocks, w_hi, w_lo, wt, gain, spread, mine, halo, coup, tb, acc, back, returned, rad_t,
     x_send, x_recv, a_send, a_recv, h_send, h_recv, b_send, b_recv, local_sem,
 ):
     box, th, ph = lax.axis_index("box"), lax.axis_index("theta"), lax.axis_index("phi")
@@ -310,13 +310,15 @@
 
     def first(i, carry):
         relay(7 - i)
+        if RELAY:
+            pl.when((i >= 2) & (lax.rem(i, 2) == 0))(functools.partial(detour, 9 - i))
         spread_out(i)
         return carry
 
     def second(i, carry):
         relay(15 - i)
         if RELAY:
-            detour(jnp.where(i < 4, 7 - 2 * i, 23 - 2 * i))
+            pl.when(lax.rem(i, 2) == 0)(functools.partial(detour, jnp.where(i == 0, 1, 17 - i)))
 
         @pl.when(i < 5)
         def _():
@@ -326,6 +328,8 @@
 
     lax.fori_loop(0, 7, first, 0)
     lax.fori_loop(0, 8, second, 0)
+    if RELAY:
+        detour(9)
 
     for m in range(4):
         rows = slice(256 * m, 256 * m + 256)
@@ -383,13 +387,16 @@
             pl.when(beside[1 - way])(shift(n, way).wait_recv)
             xb[i + 16 * way] = arrived_x[way, i]
 
-    def near(b):
+    def near(b, first_term):
         total = None
         for j in range(12):
             at = jnp.where(j < count_ref[b], ids_ref[b, j] - (rank * 8 - 8), 24)
             term = dot(stacked(blocks[b, j, 0], blocks[b, j, 1]), xb[jnp.clip(at, 0, 24)])
             total = term if j == 0 else total + term
-        out[b] = total
+        if first_term:
+            out[b] = total
+        else:
+            out[b] += total
 
     def near_pair(q):
         if q == 3:
@@ -398,7 +405,7 @@
         collect(7 - q)
 
         def one(n, carry):
-            near(q + n * (7 - 2 * q))
+            near(q + n * (7 - 2 * q), q > 1)
             return carry
 
         lax.fori_loop(0, 2, one, 0)
@@ -416,24 +423,21 @@
             device_id_type=MESH,
         ).wait_recv()
 
-    def result(o):
-        return pltpu.make_async_copy(out.at[o], out_hbm.at[o], local_sem.at[6 + o])
-
     field_re = returned[:, 0:32].reshape(512, 256)
     field_im = returned[:, 32:64].reshape(512, 256)
     for q in (3, 2, 1, 0):
-        if q < 2:
-            near_pair(q)
         rows = slice(256 * q, 256 * q + 256)
         re = dot(wt[rows, 0:512], field_re) + dot(wt[rows, 512:1024], field_re)
         im = dot(wt[rows, 0:512], field_im) + dot(wt[rows, 512:1024], field_im)
         cr, sr, ci, si = re[:128], re[128:], im[:128], im[128:]
-        leaf = jnp.concatenate([cr + si, ci - sr], axis=0).astype(BF)
-        out[q] += dot(rad_t[q], leaf)
-        result(q).start()
-        leaf = jnp.concatenate([cr - si, ci + sr], axis=0).astype(BF)
-        out[7 - q] += dot(rad_t[7 - q], leaf)
-        result(7 - q).start()
+        for o, leaf in ((q, (cr + si, ci - sr)), (7 - q, (cr - si, ci + sr))):
+            far = dot(rad_t[o], jnp.concatenate(leaf, axis=0).astype(BF))
+            if q > 1:
+                out[o] += far
+            else:
+                out[o] = far
+    for q in (1, 0):
+        near_pair(q)
 
     for i in range(8):
         for way in range(2):
@@ -446,8 +450,6 @@
             pl.when(toward[way])(pass_on(k, source_of(k // 4, k % 4), way).wait_send)
             if RELAY and k % 2:
                 pl.when(box == (15 if way == 0 else 0))(hand_over(k, source_of(k // 4, k % 4), way).wait_send)
-    for o in range(8):
-        result(o).wait()
 
 
 def per_device(coeffs, near_blocks, near_ids, near_count, radiation, partners, vector_ids, pair_count, translation):
@@ -459,7 +461,7 @@
         kernel,
         out_shape=jax.ShapeDtypeStruct((8, 256, 256), F32),
         in_specs=[smem, smem, smem, any_, any_, any_, vmem, vmem, any_, any_, vmem, any_, vmem],
-        out_specs=any_,
+        out_specs=vmem,
         scratch_shapes=[
             pltpu.VMEM((8, 2, 128, 128), BF),
             pltpu.VMEM((64, 316), BF),
@@ -481,7 +483,6 @@
             pltpu.VMEM((16, 64, 256), BF),
             pltpu.VMEM((16, 64, 256), BF),
             pltpu.VMEM((8, 256, 256), BF),
-            pltpu.VMEM((8, 256, 256), F32),
             dma((2, 8)),
             dma((2, 8)),
             dma((16,)),
@@ -490,25 +491,30 @@
             dma((2, 16)),
             dma((16,)),
             dma((16,)),
-            dma((14,)),
+            dma((6,)),
         ],
         compiler_params=pltpu.CompilerParams(
             collective_id=0, has_side_effects=True, vmem_limit_bytes=LIMIT * 1024 * 1024
         ),
     )(
-        near_ids,
-        near_count,
-        pair_count,
-        coeffs.reshape(8, 256, 256),
-        near_blocks,
-        radiation,
-        partners,
-        vector_ids,
-        table,
-        jnp.asarray(interp),
-        jnp.asarray(phase),
-        jnp.asarray(np.ascontiguousarray(interp.T)),
-        jnp.asarray(np.ascontiguousarray(phase.T)),
+        *(
+            pltpu.with_memory_space_constraint(value, pltpu.HBM)
+            for value in (
+                near_ids,
+                near_count,
+                pair_count,
+                coeffs.reshape(8, 256, 256),
+                near_blocks,
+                radiation,
+                partners,
+                vector_ids,
+                table,
+                jnp.asarray(interp),
+                jnp.asarray(phase),
+                jnp.asarray(np.ascontiguousarray(interp.T)),
+                jnp.asarray(np.ascontiguousarray(phase.T)),
+            )
+        )
     )
     return product.reshape(8, 2, 128, 256)
 

time: 58.7 us -> 54.3 us (0.925)
  Pallas kernels: 55.5 us -> 52.8 us
  local copies, waits for them, and re-layouts: 3.1 us -> 1.32 us
    pallas_call x1, Pallas kernels: 55.5 us -> 52.8 us  [per_device(): pl.pallas_call(kernel, out_shape=jax.ShapeDtypeStruct((8, 256, 256), F32)...]
    unnamed x1, local copies, waits for them, and re-layouts: 3.1 us -> 1.32 us
where the time goes in v3:
time: 54.3 us; the launch traced here: 54.1 us
  Pallas kernels  52.8 us (97%)
  local copies, waits for them, and re-layouts  1.32 us (2%)
    pallas_call x1, Pallas kernels, per_device(): pl.pallas_call(kernel, out_shape=jax.ShapeDtypeStruct((8, 256, 256), F32)...  52.8 us
    unnamed x1, local copies, waits for them, and re-layouts  1.32 us

profile of v3, /device:TPU:26, one launch (start us, length us, event | category | flops | bytes accessed | tf_op | source)
XLA Modules:
  0.0 54.1 jit_solution(6064110357294418617)
XLA Ops:
  0.0 52.8 %shard_map.127 = f32[8,256,256]{2,1,0:T(8,128)S(1)} custom-call(s32[8,12]{1,0:T(8,128)} %ids_ref.1, s32[8]{0:T(128)} %count_ref.1, s32[16]{0:T(128)} %used_ref.1, bf16[8,256,256]{2,1,0:T(8,128)(2,1)} %bitcast.6, bf16[8,12,2,128,128]{4,3,2,1,0:T(8,128)(2,1)} %blocks_hbm.1, bf16[8,2,128,128]{3,2,1,0:T(8,128)(2,1)} %rad_hbm.1, s32[16,16]{1,0:T(8,128)} %part_ref.1, ...), custom_call_target="tpu_custom_call" | custom-call | tf_op jit(solution)/shard_map/pallas_call | solution.py:460
  52.8 1.3 %copy.15 = f32[8,2,128,256]{3,2,1,0:T(8,128)} copy(f32[8,2,128,256]{3,2,1,0:T(8,128)S(1)} %bitcast.5) | data formatting | bytes 4194304

commit v4 on v3

--- a/solution.py
+++ b/solution.py
@@ -73,9 +73,9 @@
 
 
 def kernel(
-    ids_ref, count_ref, used_ref, x_hbm, blocks_hbm, rad_hbm, part_ref, vec_ref, table_hbm, interp_hbm, phase_ref,
-    interp_t_hbm, phase_t_ref, out,
-    rad_ref, table_ref, interp_ref, interp_t_ref,
+    ids_hbm, count_hbm, used_hbm, x_hbm, blocks_hbm, rad_hbm, part_hbm, vec_hbm, table_hbm, interp_hbm, phase_hbm,
+    interp_t_hbm, phase_t_hbm, out,
+    ids_ref, count_ref, used_ref, rad_ref, table_ref, interp_ref, interp_t_ref, part_ref, vec_ref, phase_ref, phase_t_ref,
     xb, arrived_x, blocks, w_hi, w_lo, wt, gain, spread, mine, halo, coup, tb, acc, back, returned, rad_t,
     x_send, x_recv, a_send, a_recv, h_send, h_recv, b_send, b_recv, local_sem,
 ):
@@ -143,8 +143,15 @@
     own_rad = load(0, rad_hbm, rad_ref)
     own_x = load(1, x_hbm, xb.at[pl.ds(8, 8)])
     own_interp = load(2, interp_hbm, interp_ref)
+    own_phase = load(8, phase_hbm, phase_ref)
     own_table = load(3, table_hbm, table_ref)
     own_interp_t = load(4, interp_t_hbm, interp_t_ref)
+    own_part = load(6, part_hbm, part_ref)
+    own_vec = load(7, vec_hbm, vec_ref)
+    own_ids = load(10, ids_hbm, ids_ref)
+    own_count = load(11, count_hbm, count_ref)
+    own_used = load(12, used_hbm, used_ref)
+    own_phase_t = load(9, phase_t_hbm, phase_t_ref)
     own_blocks = load(5, blocks_hbm, blocks)
 
     xb[24] = jnp.zeros((256, 256), BF)
@@ -240,6 +247,7 @@
             pl.when(beside[way])(shift(i, way).start)
 
     own_interp.wait()
+    own_phase.wait()
     for q in range(4):
         for part in range(2):
             cols = pl.ds((2 * q + part) * 128, 128)
@@ -263,6 +271,11 @@
         for way in range(2):
             pl.when(beside[way])(shift(i, way).start)
 
+    own_part.wait()
+    own_vec.wait()
+    own_used.wait()
+    own_ids.wait()
+    own_count.wait()
     slot = lax.broadcasted_iota(jnp.int32, (1, 16), 1)
     first_source = box * 16 - 16
     vec = jnp.concatenate([vec_ref[d : d + 1] for d in range(16)], axis=1)
@@ -339,6 +352,7 @@
         acc[rows] = total
 
     own_interp_t.wait()
+    own_phase_t.wait()
     for q in range(4):
         for part in range(2):
             rows = pl.ds((2 * q + part) * 128, 128)
@@ -460,13 +474,20 @@
     product = pl.pallas_call(
         kernel,
         out_shape=jax.ShapeDtypeStruct((8, 256, 256), F32),
-        in_specs=[smem, smem, smem, any_, any_, any_, vmem, vmem, any_, any_, vmem, any_, vmem],
+        in_specs=[any_] * 13,
         out_specs=vmem,
         scratch_shapes=[
+            pltpu.SMEM((8, 12), jnp.int32),
+            pltpu.SMEM((8,), jnp.int32),
+            pltpu.SMEM((16,), jnp.int32),
             pltpu.VMEM((8, 2, 128, 128), BF),
             pltpu.VMEM((64, 316), BF),
             pltpu.VMEM((512, 128), F32),
             pltpu.VMEM((128, 512), F32),
+            pltpu.VMEM((16, 16), jnp.int32),
+            pltpu.VMEM((16, 16), jnp.int32),
+            pltpu.VMEM((512, 8), F32),
+            pltpu.VMEM((8, 512), F32),
             pltpu.VMEM((25, 256, 256), BF),
             pltpu.VMEM((2, 8, 256, 256), BF),
             pltpu.VMEM((8, 12, 2, 128, 128), BF),
@@ -491,7 +512,7 @@
             dma((2, 16)),
             dma((16,)),
             dma((16,)),
-            dma((6,)),
+            dma((13,)),
         ],
         compiler_params=pltpu.CompilerParams(
             collective_id=0, has_side_effects=True, vmem_limit_bytes=LIMIT * 1024 * 1024

time: 54.3 us -> 53.2 us (0.980)
  Pallas kernels: 52.8 us -> 51.6 us
    pallas_call x1, Pallas kernels: 52.8 us -> 51.6 us  [per_device(): pl.pallas_call(kernel, out_shape=jax.ShapeDtypeStruct((8, 256, 256), F32)...]
where the time goes in v4:
time: 53.2 us; the launch traced here: 53 us
  Pallas kernels  51.6 us (97%)
  local copies, waits for them, and re-layouts  1.32 us (2%)
    pallas_call x1, Pallas kernels, per_device(): pl.pallas_call(kernel, out_shape=jax.ShapeDtypeStruct((8, 256, 256), F32)...  51.6 us
    unnamed x1, local copies, waits for them, and re-layouts  1.32 us

profile of v4, /device:TPU:26, one launch (start us, length us, event | category | flops | bytes accessed | tf_op | source)
XLA Modules:
  0.0 53.0 jit_solution(3499986761336075520)
XLA Ops:
  0.0 51.6 %shard_map.127 = f32[8,256,256]{2,1,0:T(8,128)S(1)} custom-call(s32[8,12]{1,0:T(8,128)} %ids_hbm.1, s32[8]{0:T(128)} %count_hbm.1, s32[16]{0:T(128)} %used_hbm.1, bf16[8,256,256]{2,1,0:T(8,128)(2,1)} %bitcast.6, bf16[8,12,2,128,128]{4,3,2,1,0:T(8,128)(2,1)} %blocks_hbm.1, bf16[8,2,128,128]{3,2,1,0:T(8,128)(2,1)} %rad_hbm.1, s32[16,16]{1,0:T(8,128)} %part_hbm.1, ...), custom_call_target="tpu_custom_call" | custom-call | tf_op jit(solution)/shard_map/pallas_call | solution.py:474
  51.6 1.3 %copy.15 = f32[8,2,128,256]{3,2,1,0:T(8,128)} copy(f32[8,2,128,256]{3,2,1,0:T(8,128)S(1)} %bitcast.5) | data formatting | bytes 4194304

commit v5 on v4

--- a/solution.py
+++ b/solution.py
@@ -17,8 +17,8 @@
 WEIGHT_UP = (-0.0546875, 0.8203125, 0.2734375, -0.0390625)
 WEIGHT_DOWN = (-0.0390625, 0.2734375, 0.8203125, -0.0546875)
 PHASE_SCALE = 1.3
-EARLY = 1
-MIDDLE = 6
+EARLY = 0
+MIDDLE = 7
 RELAY = True
 LIMIT = 40
 

time: 53.2 us -> 55.4 us (1.041)
  Pallas kernels: 51.6 us -> 54 us
    pallas_call x1, Pallas kernels: 51.6 us -> 54 us  [per_device(): pl.pallas_call(kernel, out_shape=jax.ShapeDtypeStruct((8, 256, 256), F32)...]
where the time goes in v5:
time: 55.4 us
  Pallas kernels  54 us (97%)
  local copies, waits for them, and re-layouts  1.32 us (2%)
    pallas_call x1, Pallas kernels, per_device(): pl.pallas_call(kernel, out_shape=jax.ShapeDtypeStruct((8, 256, 256), F32)...  54 us
    unnamed x1, local copies, waits for them, and re-layouts  1.32 us

profile of v5, /device:TPU:26, one launch (start us, length us, event | category | flops | bytes accessed | tf_op | source)
XLA Modules:
  0.0 55.4 jit_solution(2002905067537370557)
XLA Ops:
  0.0 54.0 %shard_map.127 = f32[8,256,256]{2,1,0:T(8,128)S(1)} custom-call(s32[8,12]{1,0:T(8,128)} %ids_hbm.1, s32[8]{0:T(128)} %count_hbm.1, s32[16]{0:T(128)} %used_hbm.1, bf16[8,256,256]{2,1,0:T(8,128)(2,1)} %bitcast.6, bf16[8,12,2,128,128]{4,3,2,1,0:T(8,128)(2,1)} %blocks_hbm.1, bf16[8,2,128,128]{3,2,1,0:T(8,128)(2,1)} %rad_hbm.1, s32[16,16]{1,0:T(8,128)} %part_hbm.1, ...), custom_call_target="tpu_custom_call" | custom-call | tf_op jit(solution)/shard_map/pallas_call | solution.py:474
  54.0 1.3 %copy.15 = f32[8,2,128,256]{3,2,1,0:T(8,128)} copy(f32[8,2,128,256]{3,2,1,0:T(8,128)S(1)} %bitcast.5) | data formatting | bytes 4194304
